TPU v7x, 256 devices: a whole 4x4x8 slice. The times are simulated.
256 devices in a mesh: pulse: 8 (over y, core), tile: 32 (over x, z).
Axes of the slice: x: 4, y: 4, z: 8, core: 2. Of those that a mesh axis runs over, the one named last changes fastest.
Arguments:
- echoes: bfloat16 [512, 2, 2, 16384], P(('pulse', 'tile')), may hold values from -6 to 6
- pulse_slope: bfloat16 [512, 2], P(('pulse', 'tile')), may hold values from -0.023925781 to 0.023925781
- pulse_shift: bfloat16 [512, 2], P(('pulse', 'tile')), may hold values from -3.140625 to 3.140625
- footprint: int32 [8, 32, 32], P('pulse'), may hold values from -1 to 63, as said below
- band_start: int32 [1024], P('tile'), may hold values from 0 to 13216
- row_phase: float32 [1024], P('tile'), may hold values from -1 to 1
Outputs:
- formed_image: float32 [2, 1024, 4096], P(None, 'tile', 'pulse')
Inputs may be any that keep to these rules, and one draw needn't show every extreme that they name: footprint[g, t] lists in rising order the numbers of group g's blocks whose echoes reach row strip t, then -1 to the end. It names at most one block of each run of 2 numbers that starts at a multiple of 2. In every group some list has 32 entries.
All inputs are finite; a program needn't handle non-finite values.
Results may differ from a plain program's by a relative error of at most 0.0039.
Values may be sent and summed in bfloat16 or wider, within the bound.
No kernel may reach another device: no remote copies, remote signals or barrier semaphores. Data moves between devices by JAX's collectives and lax.ppermute only.
A program may use at most 64 MiB of HBM per device.

v0:
```python
import jax
import jax.numpy as jnp
from jax import lax
from jax.sharding import PartitionSpec as P

NCOL = 4096
PB = 2
ITERS = 2
step_size = 0.5
tv_weight = 0.4
floor_square = 0.25


def padded_2(value, sides, width):
    for axis, dim in sides:
        size, length = (lax.axis_size(axis), value.shape[dim])
        up = [(i, (i + 1) % size) for i in range(size - 1)]
        down = [(j, i) for i, j in up]
        last = lax.slice_in_dim(value, length - width, length, axis=dim)
        leading = lax.slice_in_dim(value, 0, width, axis=dim)
        before = lax.ppermute(last, axis, up)
        after = lax.ppermute(leading, axis, down)
        value = jnp.concatenate([before, value, after], axis=dim)
    return value


def cubic_table():
    columns = jnp.arange(128, dtype=jnp.int32)
    quarter_pos = 3 * columns + 4
    base_tap = quarter_pos // 4
    fraction = (quarter_pos % 4).astype(jnp.float32) / 4.0
    fraction_sq = fraction * fraction
    fraction_cube = fraction_sq * fraction
    weights = [
        (-fraction_cube + 2.0 * fraction_sq - fraction) * 0.5,
        (3.0 * fraction_cube - 5.0 * fraction_sq + 2.0) * 0.5,
        (-3.0 * fraction_cube + 4.0 * fraction_sq + fraction) * 0.5,
        (fraction_cube - fraction_sq) * 0.5,
    ]
    tap_rows = jnp.arange(128, dtype=jnp.int32)[:, None]
    cubic_weights = jnp.zeros((128, 128), jnp.float32)
    for tap_shift, weight in zip(range(-1, 3), weights):
        cubic_weights = cubic_weights + jnp.where(
            tap_rows == (base_tap + tap_shift)[None, :], weight[None, :], 0.0
        )
    return cubic_weights


def block_image(block_echo, block_slope, block_shift, band_start, row_phase, cubic_weights):
    pulses = block_echo.shape[0]
    row_count = band_start.shape[0]
    col_blocks = NCOL // 128
    window_span = 96 * (col_blocks + 1)
    flat_echo = block_echo.reshape(pulses * 2, block_echo.shape[2])
    segments = jax.vmap(
        lambda row_start: lax.dynamic_slice_in_dim(flat_echo, row_start, window_span, axis=1)
    )(band_start)
    leading = segments[..., : 96 * col_blocks].reshape(row_count, pulses * 2, col_blocks, 96)
    trailing = segments[..., 96:].reshape(row_count, pulses * 2, col_blocks, 96)[..., :32]
    windows = jnp.concatenate([leading, trailing], axis=-1)
    windows = (
        jnp.transpose(windows, (0, 2, 1, 3))
        .reshape(row_count, col_blocks, pulses, 2, 128)
        .astype(jnp.float32)
    )
    slopes = block_slope.astype(jnp.float32)
    shifts = block_shift.astype(jnp.float32)
    block_pos = (128 * jnp.arange(col_blocks, dtype=jnp.int32)).astype(jnp.float32)
    angle_grid = (
        shifts[None, None, :] * row_phase[:, None, None]
        + slopes[None, None, :] * block_pos[None, :, None]
    )
    cosine = jnp.cos(angle_grid)[..., None]
    sines = jnp.sin(angle_grid)[..., None]
    real_part = windows[:, :, :, 0]
    imag_part = windows[:, :, :, 1]
    turned_re = real_part * cosine - imag_part * sines
    turned_im = real_part * sines + imag_part * cosine
    turned = (
        jnp.stack([turned_re, turned_im], axis=3)
        .astype(jnp.bfloat16)
        .reshape(row_count * col_blocks, pulses * 256)
    )
    column_pos = jnp.arange(128, dtype=jnp.int32).astype(jnp.float32)
    column_ramp = slopes[:, None] * column_pos[None, :]
    kernel_re = cubic_weights[None] * jnp.cos(column_ramp)[:, None, :]
    kernel_im = cubic_weights[None] * jnp.sin(column_ramp)[:, None, :]
    upper_rows = jnp.concatenate([kernel_re, kernel_im], axis=2)
    bottom = jnp.concatenate([-kernel_im, kernel_re], axis=2)
    kernel = jnp.stack([upper_rows, bottom], axis=1).astype(jnp.bfloat16).reshape(pulses * 256, 256)
    product = jnp.dot(turned, kernel, preferred_element_type=jnp.float32)
    return product.reshape(row_count, col_blocks, 256)


def add_used(
    running, echo_all, slope_all, shift_all, slots, used_count, band_start, row_phase, cubic_weights
):
    slot_count = slots.shape[0]

    def add_pair(pair_index, partial_sum):
        first_slot = slots[2 * pair_index]
        second_slot = slots[jnp.minimum(2 * pair_index + 1, slot_count - 1)]
        second_used = 2 * pair_index + 1 < used_count
        second_echo = jnp.where(second_used, echo_all[second_slot], jnp.zeros_like(echo_all[0]))
        echo_pair = jnp.concatenate([echo_all[first_slot], second_echo], axis=0)
        slope_pair = jnp.concatenate([slope_all[first_slot], slope_all[second_slot]], axis=0)
        shift_pair = jnp.concatenate([shift_all[first_slot], shift_all[second_slot]], axis=0)
        return partial_sum + block_image(
            echo_pair, slope_pair, shift_pair, band_start, row_phase, cubic_weights
        )

    return lax.fori_loop(0, (used_count + 1) // 2, add_pair, running)


def tv_update(field, padded, base_image, row_anchor, col_anchor, grid_rows, grid_cols):
    row_count = field.shape[1]
    col_count = field.shape[2]
    grad_rows = (
        padded[:, 1 : row_count + 2, 0 : col_count + 1]
        - padded[:, 0 : row_count + 1, 0 : col_count + 1]
    )
    grad_cols = (
        padded[:, 0 : row_count + 1, 1 : col_count + 2]
        - padded[:, 0 : row_count + 1, 0 : col_count + 1]
    )
    row_ids = row_anchor - 1 + jnp.arange(row_count + 1, dtype=jnp.int32)
    col_ids = col_anchor - 1 + jnp.arange(col_count + 1, dtype=jnp.int32)
    inside = (row_ids >= 0)[:, None] & (col_ids >= 0)[None, :]
    grad_rows = jnp.where((inside & (row_ids < grid_rows - 1)[:, None])[None], grad_rows, 0.0)
    grad_cols = jnp.where((inside & (col_ids < grid_cols - 1)[None, :])[None], grad_cols, 0.0)
    magnitude = jnp.sqrt(
        jnp.sum(grad_rows * grad_rows + grad_cols * grad_cols, axis=0) + floor_square
    )
    flux_rows = grad_rows / magnitude[None]
    flux_cols = grad_cols / magnitude[None]
    divergence = (
        flux_rows[:, 1:, 1:] - flux_rows[:, :-1, 1:] + flux_cols[:, 1:, 1:] - flux_cols[:, 1:, :-1]
    )
    return field - step_size * (field - base_image - tv_weight * divergence)


def to_image(blocks):
    row_count = blocks.shape[0]
    col_count = blocks.shape[1] * 128
    real_plane = blocks[..., :128].reshape(row_count, col_count)
    imag_plane = blocks[..., 128:].reshape(row_count, col_count)
    return jnp.stack([real_plane, imag_plane])


def body(echoes, pulse_slope, pulse_shift, footprint, band_start, row_phase):
    tile_count = lax.axis_size("tile")
    groups = lax.axis_size("pulse")
    tile_index = lax.axis_index("tile")
    group_index = lax.axis_index("pulse")
    row_count = band_start.shape[0]
    col_blocks = NCOL // 128
    cubic_weights = cubic_table()
    footprints = footprint[0]
    own_list = lax.dynamic_index_in_dim(footprints, tile_index, axis=0, keepdims=False)
    zero_image = jnp.zeros((row_count, col_blocks, 256), jnp.float32)
    piece_echo = lax.all_gather(echoes, "tile", axis=0, tiled=True)
    piece_slope = lax.all_gather(pulse_slope, "tile", axis=0, tiled=True)
    piece_shift = lax.all_gather(pulse_shift, "tile", axis=0, tiled=True)
    piece_count = piece_echo.shape[0]
    positions = jnp.arange(piece_count, dtype=jnp.int32)
    is_used = jnp.any(positions[:, None] == own_list[None, :], axis=1)
    ordering = jnp.argsort(jnp.where(is_used, 0, piece_count) + positions)
    used_total = jnp.sum(is_used.astype(jnp.int32))
    partial_image = add_used(
        zero_image,
        piece_echo,
        piece_slope,
        piece_shift,
        ordering,
        used_total,
        band_start,
        row_phase,
        cubic_weights,
    )
    normalize = float(PB * tile_count * groups) ** (-0.5)
    grid_rows = tile_count * row_count
    row_anchor = tile_index * row_count
    whole = lax.psum(partial_image, "pulse")
    base_image = to_image(whole) * normalize
    field = base_image
    for iteration in range(ITERS):
        padded = padded_2(field, (("tile", 1),), 1)
        padded = jnp.pad(padded, ((0, 0), (0, 0), (1, 1)))
        field = tv_update(field, padded, base_image, row_anchor, 0, grid_rows, NCOL)
    share_width = NCOL // groups
    return lax.dynamic_slice_in_dim(field, group_index * share_width, share_width, axis=2)


def solution(mesh):
    in_specs = (
        P(("pulse", "tile"), None, None, None),
        P(("pulse", "tile"), None),
        P(("pulse", "tile"), None),
        P("pulse", None, None),
        P("tile"),
        P("tile"),
    )
    out_specs = P(None, "tile", "pulse")
    return jax.shard_map(body, mesh=mesh, in_specs=in_specs, out_specs=out_specs, check_vma=False)
```

profile of v0, /device:TPU:64, one launch (start us, length us, event | category | flops | bytes accessed | tf_op | source)
XLA Modules:
  0.0 1211.1 jit_solution(6912679305393457067)
XLA Ops:
  8.7 2.0 sort.17
  10.7 40.3 %all-gather = bf16[32,2,2]{2,1,0:T(2,128)(2,1)S(1)} all-gather(bf16[1,2,2]{2,1,0:T(2,128)(2,1)} %bitcast.74), channel_id=1, replica_groups=mesh['pulse'=8,'tile'=32] {'tile'}, dimensions={0}, use_global_device_ids=true | all-gather | bytes 264 | tf_op jit(solution)/shard_map/all_gather | solution.py:163
  51.0 37.3 %all-gather.1 = bf16[32,2,2]{2,1,0:T(2,128)(2,1)S(1)} all-gather(bf16[1,2,2]{2,1,0:T(2,128)(2,1)} %bitcast.75), channel_id=1, replica_groups=mesh['pulse'=8,'tile'=32] {'tile'}, dimensions={0}, use_global_device_ids=true | all-gather | bytes 264 | tf_op jit(solution)/shard_map/all_gather | solution.py:162
  88.4 20.5 %all-gather.4.cloned.1.call-done = bf16[64,2,2,16384]{3,2,1,0:T(2,128)(2,1)} async-done(((bf16[2,2,2,16384]{3,2,1,0:T(2,128)(2,1)}), bf16[64,2,2,16384]{3,2,1,0:T(2,128)(2,1)}) %all-gather.4.cloned.1.call-update) | async-done | bytes 8388624 | tf_op jit(solution)/shard_map/all_gather | solution.py:161
  109.1 437.2 %while.17 = (s32[]{:T(128)}, f32[32,32,256]{2,1,0:T(8,128)S(1)}, s32[]{:T(128)}, s32[64]{0:T(128)S(1)}, bf16[64,2,2,16384]{3,2,1,0:T(2,128)(2,1)}, /*index=5*/s3...) while((s32[]{:T(128)}, f32[32,32,256]{2,1,0:T(8,128)S(1)}, ...), condition=%wide.region_4.5_spmd.clone.clone, body=%wide.region_3.4_spmd.clone.clone.sunk | while | flops 548656192 | bytes 41472712 | solution.py:112
  115.5 39.0 %while.18 = (s32[]{:T(128)}, bf16[8,16384]{1,0:T(8,128)(2,1)S(1)}, s32[32,2]{0,1:T(2,128)S(1)}, bf16[32,8,3168]{2,1,0:T(8,128)(2,1)S(1)}, s32[]{:T(128)}) while((s32[]{:T(128)}, bf16[8,16384]{1,0:T(8,128)(2,1)S(1)}, s32[32,2]{0,1:T(2,128)S(1)}, bf16[32,8,3168]{2,1,0:T(8,128)(2,1)S(1)}, s32[]{:T(128)}) %tuple.94), condition=%wide.while_cond, body=%wide.while_body.sunk | while | flops 2 | bytes 102497 | solution.py:56
  154.5 2.4 fusion.59
  157.0 3.6 reshape.426
  160.6 4.5 reshape.427
  165.1 2.6 maximum_convert_fusion.6
  169.0 1.4 subtract_convert_fusion.2
  178.0 39.0 %while.18 = (s32[]{:T(128)}, bf16[8,16384]{1,0:T(8,128)(2,1)S(1)}, s32[32,2]{0,1:T(2,128)S(1)}, bf16[32,8,3168]{2,1,0:T(8,128)(2,1)S(1)}, s32[]{:T(128)}) while((s32[]{:T(128)}, bf16[8,16384]{1,0:T(8,128)(2,1)S(1)}, s32[32,2]{0,1:T(2,128)S(1)}, bf16[32,8,3168]{2,1,0:T(8,128)(2,1)S(1)}, s32[]{:T(128)}) %tuple.94), condition=%wide.while_cond, body=%wide.while_body.sunk | while | flops 2 | bytes 102497 | solution.py:56
  217.0 2.4 fusion.59
  219.4 3.6 reshape.426
  223.0 4.5 reshape.427
  227.6 2.6 maximum_convert_fusion.6
  240.4 39.0 %while.18 = (s32[]{:T(128)}, bf16[8,16384]{1,0:T(8,128)(2,1)S(1)}, s32[32,2]{0,1:T(2,128)S(1)}, bf16[32,8,3168]{2,1,0:T(8,128)(2,1)S(1)}, s32[]{:T(128)}) while((s32[]{:T(128)}, bf16[8,16384]{1,0:T(8,128)(2,1)S(1)}, s32[32,2]{0,1:T(2,128)S(1)}, bf16[32,8,3168]{2,1,0:T(8,128)(2,1)S(1)}, s32[]{:T(128)}) %tuple.94), condition=%wide.while_cond, body=%wide.while_body.sunk | while | flops 2 | bytes 102497 | solution.py:56
  279.4 2.4 fusion.59
  281.9 3.6 reshape.426
  285.5 4.5 reshape.427
  290.0 2.6 maximum_convert_fusion.6
  302.9 39.0 %while.18 = (s32[]{:T(128)}, bf16[8,16384]{1,0:T(8,128)(2,1)S(1)}, s32[32,2]{0,1:T(2,128)S(1)}, bf16[32,8,3168]{2,1,0:T(8,128)(2,1)S(1)}, s32[]{:T(128)}) while((s32[]{:T(128)}, bf16[8,16384]{1,0:T(8,128)(2,1)S(1)}, s32[32,2]{0,1:T(2,128)S(1)}, bf16[32,8,3168]{2,1,0:T(8,128)(2,1)S(1)}, s32[]{:T(128)}) %tuple.94), condition=%wide.while_cond, body=%wide.while_body.sunk | while | flops 2 | bytes 102497 | solution.py:56
  341.9 2.4 fusion.59
  344.3 3.6 reshape.426
  347.9 4.5 reshape.427
  352.5 2.6 maximum_convert_fusion.6
  365.3 39.0 %while.18 = (s32[]{:T(128)}, bf16[8,16384]{1,0:T(8,128)(2,1)S(1)}, s32[32,2]{0,1:T(2,128)S(1)}, bf16[32,8,3168]{2,1,0:T(8,128)(2,1)S(1)}, s32[]{:T(128)}) while((s32[]{:T(128)}, bf16[8,16384]{1,0:T(8,128)(2,1)S(1)}, s32[32,2]{0,1:T(2,128)S(1)}, bf16[32,8,3168]{2,1,0:T(8,128)(2,1)S(1)}, s32[]{:T(128)}) %tuple.94), condition=%wide.while_cond, body=%wide.while_body.sunk | while | flops 2 | bytes 102497 | solution.py:56
  404.4 2.4 fusion.59
  406.8 3.6 reshape.426
  410.4 4.5 reshape.427
  414.9 2.6 maximum_convert_fusion.6
  427.8 39.0 %while.18 = (s32[]{:T(128)}, bf16[8,16384]{1,0:T(8,128)(2,1)S(1)}, s32[32,2]{0,1:T(2,128)S(1)}, bf16[32,8,3168]{2,1,0:T(8,128)(2,1)S(1)}, s32[]{:T(128)}) while((s32[]{:T(128)}, bf16[8,16384]{1,0:T(8,128)(2,1)S(1)}, s32[32,2]{0,1:T(2,128)S(1)}, bf16[32,8,3168]{2,1,0:T(8,128)(2,1)S(1)}, s32[]{:T(128)}) %tuple.94), condition=%wide.while_cond, body=%wide.while_body.sunk | while | flops 2 | bytes 102497 | solution.py:56
  466.8 2.4 fusion.59
  469.2 3.6 reshape.426
  472.8 4.5 reshape.427
  477.4 2.6 maximum_convert_fusion.6
  490.2 39.0 %while.18 = (s32[]{:T(128)}, bf16[8,16384]{1,0:T(8,128)(2,1)S(1)}, s32[32,2]{0,1:T(2,128)S(1)}, bf16[32,8,3168]{2,1,0:T(8,128)(2,1)S(1)}, s32[]{:T(128)}) while((s32[]{:T(128)}, bf16[8,16384]{1,0:T(8,128)(2,1)S(1)}, s32[32,2]{0,1:T(2,128)S(1)}, bf16[32,8,3168]{2,1,0:T(8,128)(2,1)S(1)}, s32[]{:T(128)}) %tuple.94), condition=%wide.while_cond, body=%wide.while_body.sunk | while | flops 2 | bytes 102497 | solution.py:56
  529.3 2.4 fusion.59
  531.7 3.6 reshape.426
  535.3 4.5 reshape.427
  539.8 2.6 maximum_convert_fusion.6
  547.3 627.9 %all-reduce.5.cloned.1.call-done = f32[32,32,256]{2,1,0:T(8,128)} async-done(((f32[32,32,256]{2,1,0:T(8,128)}), f32[32,32,256]{2,1,0:T(8,128)}) %all-reduce.5.cloned.1.call-update) | async-done | bytes 1048592 | tf_op jit(solution)/shard_map/psum | solution.py:183
  1176.8 3.5 collective-permute-start
  1180.3 2.4 collective-permute-start.1
  1183.0 3.9 collective-permute-done.1
  1189.7 5.1 collective-permute-start.2
  1194.9 2.1 collective-permute-start.3
  1197.0 3.7 collective-permute-done.3
  (869 shorter events, 320.4 us)
Async XLA Ops:
  6.5 0.8 copy-start
  6.5 102.5 %copy-start.3 = (s32[32]{0:T(128)S(1)}, s32[32]{0:T(128)}, u32[]{:S(2)}) copy-start(s32[32]{0:T(128)} %param.12) | copy-start | bytes 388
  6.5 102.5 %copy-start.2 = (f32[32]{0:T(128)S(1)}, f32[32]{0:T(128)}, u32[]{:S(2)}) copy-start(f32[32]{0:T(128)} %param.13) | copy-start | bytes 388
  6.5 102.4 %all-gather.4.cloned.1.call-start = ((), (), s32[]{:S(2)}) async-start(), calls=%async_computation | async-start | bytes 8650752 | tf_op jit(solution)/shard_map/all_gather | solution.py:161
  7.3 1167.9 %all-reduce.5.cloned.1.call-start = ((), (), s32[]{:S(2)}) async-start(), calls=%async_computation.1 | async-start | bytes 2097152 | tf_op jit(solution)/shard_map/psum | solution.py:183
  546.3 1.0 copy-start.1
  1176.8 6.1 collective-permute-start
  1180.3 6.6 collective-permute-start.1
  1189.7 7.3 collective-permute-start.2
  1194.9 5.8 collective-permute-start.3
Sparse Core Ops, SparseCore 0:
  9.9 98.9 all-gather.3
  547.4 627.7 all-reduce.4
where the time goes:
time: 1220 us; the launch traced here: 1210 us
  waiting for transfers between devices  657 us (54%)
  local copies, waits for them, and re-layouts  356 us (29%)
  blocking collectives  77.7 us (6%)
  other arithmetic  54.3 us (4%)
  loops' own time  33.9 us (3%)
  between operations  14.2 us (1%)
  starting transfers between devices  13.1 us (1%)
    psum x1, waiting for transfers between devices, body(): whole = lax.psum(partial_image, 'pulse')  628 us
    gather x672, local copies, waits for them, and re-layouts  269 us
    all_gather x1, blocking collectives, body(): piece_shift = lax.all_gather(pulse_shift, 'tile', axis=0, tiled=True)  40.3 us
    all_gather x1, blocking collectives, body(): piece_slope = lax.all_gather(pulse_slope, 'tile', axis=0, tiled=True)  37.3 us
    reshape x7, local copies, waits for them, and re-layouts, block_image(): segments[..., :96 * col_blocks]  31.8 us
    another operation x1, loops' own time, add_used(): return lax.fori_loop(0, (used_count + 1) // 2, add_pair, running)  29.9 us
    reshape x7, local copies, waits for them, and re-layouts, block_image(): segments[..., 96:].reshape(row_count, pulses * 2, col_blocks, 96)[..., :32]  25.1 us
  transfers between devices with their start and end apart: 6, of which 4 were waited for; matrix products, arithmetic and copies ran while one was open for 0% of the time, Pallas kernels for 0%

commit v1 on v0

--- a/solution.py
+++ b/solution.py
@@ -180,7 +180,9 @@
     normalize = float(PB * tile_count * groups) ** (-0.5)
     grid_rows = tile_count * row_count
     row_anchor = tile_index * row_count
-    whole = lax.psum(partial_image, "pulse")
+    whole = partial_image
+    for hop in (1, 2, 4):
+        whole = whole + lax.ppermute(whole, "pulse", [(dev, dev ^ hop) for dev in range(8)])
     base_image = to_image(whole) * normalize
     field = base_image
     for iteration in range(ITERS):

time: 1220 us -> 1300 us (1.066)
  starting transfers between devices: 13.1 us -> 151 us
  waiting for transfers between devices: 657 us -> 557 us
  local copies, waits for them, and re-layouts: 356 us -> 391 us
    psum x1 -> x0, waiting for transfers between devices: 628 us -> none  [body(): whole = lax.psum(partial_image, 'pulse')]
    ppermute x2, waiting for transfers between devices: 7.6 us -> 483 us  [padded_2(): after = lax.ppermute(leading, axis, down)]
    ppermute x0 -> x3, starting transfers between devices: none -> 138 us  [body(): lax.ppermute(whole, 'pulse', [(dev, dev ^ hop) for dev in range(8)])]
    ppermute x0 -> x3, waiting for transfers between devices: none -> 52.2 us  [body(): lax.ppermute(whole, 'pulse', [(dev, dev ^ hop) for dev in range(8)])]
    gather x672, local copies, waits for them, and re-layouts: 269 us -> 306 us
  transfers between devices with their start and end apart: 6 -> 8, of which waited for: 4 -> 6; matrix products, arithmetic and copies ran while one was open for 0% -> 0% of each run, Pallas kernels for 0% -> 0%
where the time goes in v1:
time: 1300 us; the launch traced here: 1290 us
  waiting for transfers between devices  557 us (43%)
  local copies, waits for them, and re-layouts  391 us (30%)
  starting transfers between devices  151 us (12%)
  blocking collectives  77.6 us (6%)
  other arithmetic  55 us (4%)
  loops' own time  36.9 us (3%)
  between operations  14.3 us (1%)
    ppermute x2, waiting for transfers between devices, padded_2(): after = lax.ppermute(leading, axis, down)  483 us
    gather x672, local copies, waits for them, and re-layouts  306 us
    ppermute x3, starting transfers between devices, body(): lax.ppermute(whole, 'pulse', [(dev, dev ^ hop) for dev in range(8)])  138 us
    ppermute x3, waiting for transfers between devices, body(): lax.ppermute(whole, 'pulse', [(dev, dev ^ hop) for dev in range(8)])  52.2 us
    all_gather x1, blocking collectives, body(): piece_shift = lax.all_gather(pulse_shift, 'tile', axis=0, tiled=True)  40.3 us
    all_gather x1, blocking collectives, body(): piece_slope = lax.all_gather(pulse_slope, 'tile', axis=0, tiled=True)  37.3 us
    another operation x1, loops' own time, add_used(): return lax.fori_loop(0, (used_count + 1) // 2, add_pair, running)  32.9 us
    reshape x7, local copies, waits for them, and re-layouts, block_image(): segments[..., :96 * col_blocks]  31.8 us
  transfers between devices with their start and end apart: 8, of which 6 were waited for; matrix products, arithmetic and copies ran while one was open for 0% of the time, Pallas kernels for 0%

profile of v1, /device:TPU:64, one launch (start us, length us, event | category | flops | bytes accessed | tf_op | source)
XLA Modules:
  0.0 1288.2 jit_solution(17654226696622599456)
XLA Ops:
  10.8 40.3 %all-gather = bf16[32,2,2]{2,1,0:T(2,128)(2,1)S(1)} all-gather(bf16[1,2,2]{2,1,0:T(2,128)(2,1)} %bitcast.74), channel_id=1, replica_groups=mesh['pulse'=8,'tile'=32] {'tile'}, dimensions={0}, use_global_device_ids=true | all-gather | bytes 264 | tf_op jit(solution)/shard_map/all_gather | solution.py:163
  51.1 37.3 %all-gather.1 = bf16[32,2,2]{2,1,0:T(2,128)(2,1)S(1)} all-gather(bf16[1,2,2]{2,1,0:T(2,128)(2,1)} %bitcast.75), channel_id=1, replica_groups=mesh['pulse'=8,'tile'=32] {'tile'}, dimensions={0}, use_global_device_ids=true | all-gather | bytes 264 | tf_op jit(solution)/shard_map/all_gather | solution.py:162
  88.5 20.5 %all-gather.4.cloned.1.call-done = bf16[64,2,2,16384]{3,2,1,0:T(2,128)(2,1)} async-done(((bf16[2,2,2,16384]{3,2,1,0:T(2,128)(2,1)}), bf16[64,2,2,16384]{3,2,1,0:T(2,128)(2,1)}) %all-gather.4.cloned.1.call-update) | async-done | bytes 8388624 | tf_op jit(solution)/shard_map/all_gather | solution.py:161
  109.1 477.6 %while.17 = (s32[]{:T(128)}, f32[32,32,256]{2,1,0:T(8,128)S(1)}, s32[]{:T(128)}, s32[64]{0:T(128)S(1)}, bf16[64,2,2,16384]{3,2,1,0:T(2,128)(2,1)}, /*index=5*/s3...) while((s32[]{:T(128)}, f32[32,32,256]{2,1,0:T(8,128)S(1)}, ...), condition=%wide.region_4.5_spmd.clone.clone, body=%wide.region_3.4_spmd.clone.clone.sunk | while | flops 548656192 | bytes 41472712 | solution.py:112
  116.0 44.3 %while.18 = (s32[]{:T(128)}, bf16[8,16384]{1,0:T(8,128)(2,1)S(1)}, s32[32,2]{0,1:T(2,128)S(1)}, bf16[32,8,3168]{2,1,0:T(8,128)(2,1)S(1)}, s32[]{:T(128)}) while((s32[]{:T(128)}, bf16[8,16384]{1,0:T(8,128)(2,1)S(1)}, s32[32,2]{0,1:T(2,128)S(1)}, bf16[32,8,3168]{2,1,0:T(8,128)(2,1)S(1)}, s32[]{:T(128)}) %tuple.94), condition=%wide.while_cond, body=%wide.while_body.sunk | while | flops 2 | bytes 102497 | solution.py:56
  160.3 2.4 fusion.59
  162.8 3.6 reshape.426
  166.4 4.5 reshape.427
  170.9 2.6 maximum_convert_fusion.6
  184.2 44.3 %while.18 = (s32[]{:T(128)}, bf16[8,16384]{1,0:T(8,128)(2,1)S(1)}, s32[32,2]{0,1:T(2,128)S(1)}, bf16[32,8,3168]{2,1,0:T(8,128)(2,1)S(1)}, s32[]{:T(128)}) while((s32[]{:T(128)}, bf16[8,16384]{1,0:T(8,128)(2,1)S(1)}, s32[32,2]{0,1:T(2,128)S(1)}, bf16[32,8,3168]{2,1,0:T(8,128)(2,1)S(1)}, s32[]{:T(128)}) %tuple.94), condition=%wide.while_cond, body=%wide.while_body.sunk | while | flops 2 | bytes 102497 | solution.py:56
  228.5 2.4 fusion.59
  231.0 3.6 reshape.426
  234.6 4.5 reshape.427
  239.1 2.6 maximum_convert_fusion.6
  252.4 44.3 %while.18 = (s32[]{:T(128)}, bf16[8,16384]{1,0:T(8,128)(2,1)S(1)}, s32[32,2]{0,1:T(2,128)S(1)}, bf16[32,8,3168]{2,1,0:T(8,128)(2,1)S(1)}, s32[]{:T(128)}) while((s32[]{:T(128)}, bf16[8,16384]{1,0:T(8,128)(2,1)S(1)}, s32[32,2]{0,1:T(2,128)S(1)}, bf16[32,8,3168]{2,1,0:T(8,128)(2,1)S(1)}, s32[]{:T(128)}) %tuple.94), condition=%wide.while_cond, body=%wide.while_body.sunk | while | flops 2 | bytes 102497 | solution.py:56
  296.8 2.4 fusion.59
  299.2 3.6 reshape.426
  302.8 4.5 reshape.427
  307.3 2.6 maximum_convert_fusion.6
  320.6 44.3 %while.18 = (s32[]{:T(128)}, bf16[8,16384]{1,0:T(8,128)(2,1)S(1)}, s32[32,2]{0,1:T(2,128)S(1)}, bf16[32,8,3168]{2,1,0:T(8,128)(2,1)S(1)}, s32[]{:T(128)}) while((s32[]{:T(128)}, bf16[8,16384]{1,0:T(8,128)(2,1)S(1)}, s32[32,2]{0,1:T(2,128)S(1)}, bf16[32,8,3168]{2,1,0:T(8,128)(2,1)S(1)}, s32[]{:T(128)}) %tuple.94), condition=%wide.while_cond, body=%wide.while_body.sunk | while | flops 2 | bytes 102497 | solution.py:56
  365.0 2.4 fusion.59
  367.4 3.6 reshape.426
  371.0 4.5 reshape.427
  375.6 2.6 maximum_convert_fusion.6
  388.9 44.3 %while.18 = (s32[]{:T(128)}, bf16[8,16384]{1,0:T(8,128)(2,1)S(1)}, s32[32,2]{0,1:T(2,128)S(1)}, bf16[32,8,3168]{2,1,0:T(8,128)(2,1)S(1)}, s32[]{:T(128)}) while((s32[]{:T(128)}, bf16[8,16384]{1,0:T(8,128)(2,1)S(1)}, s32[32,2]{0,1:T(2,128)S(1)}, bf16[32,8,3168]{2,1,0:T(8,128)(2,1)S(1)}, s32[]{:T(128)}) %tuple.94), condition=%wide.while_cond, body=%wide.while_body.sunk | while | flops 2 | bytes 102497 | solution.py:56
  433.2 2.4 fusion.59
  435.7 3.6 reshape.426
  439.3 4.5 reshape.427
  443.8 2.6 maximum_convert_fusion.6
  457.1 44.3 %while.18 = (s32[]{:T(128)}, bf16[8,16384]{1,0:T(8,128)(2,1)S(1)}, s32[32,2]{0,1:T(2,128)S(1)}, bf16[32,8,3168]{2,1,0:T(8,128)(2,1)S(1)}, s32[]{:T(128)}) while((s32[]{:T(128)}, bf16[8,16384]{1,0:T(8,128)(2,1)S(1)}, s32[32,2]{0,1:T(2,128)S(1)}, bf16[32,8,3168]{2,1,0:T(8,128)(2,1)S(1)}, s32[]{:T(128)}) %tuple.94), condition=%wide.while_cond, body=%wide.while_body.sunk | while | flops 2 | bytes 102497 | solution.py:56
  501.4 2.4 fusion.59
  503.9 3.6 reshape.426
  507.5 4.5 reshape.427
  512.0 2.6 maximum_convert_fusion.6
  525.3 44.3 %while.18 = (s32[]{:T(128)}, bf16[8,16384]{1,0:T(8,128)(2,1)S(1)}, s32[32,2]{0,1:T(2,128)S(1)}, bf16[32,8,3168]{2,1,0:T(8,128)(2,1)S(1)}, s32[]{:T(128)}) while((s32[]{:T(128)}, bf16[8,16384]{1,0:T(8,128)(2,1)S(1)}, s32[32,2]{0,1:T(2,128)S(1)}, bf16[32,8,3168]{2,1,0:T(8,128)(2,1)S(1)}, s32[]{:T(128)}) %tuple.94), condition=%wide.while_cond, body=%wide.while_body.sunk | while | flops 2 | bytes 102497 | solution.py:56
  569.7 2.4 fusion.59
  572.1 3.6 reshape.426
  575.7 4.5 reshape.427
  580.3 2.6 maximum_convert_fusion.6
  586.8 2.6 collective-permute-done
  589.6 138.0 %collective-permute-start.1 = (f32[32,32,256]{2,1,0:T(8,128)S(1)}, f32[32,32,256]{2,1,0:T(8,128)S(1)}, u32[]{:S(2)}, u32[]{:S(2)}) collective-permute-start(f32[32,32,256]{2,1,0:T(8,128)S(1)} %add.309), channel_id=1, source_target_pairs={{0,64},{32,96},{64,0},{96,32},{128,192},{160,224},{192,128},{224,1... | collective-permute-start | bytes 3145736 | tf_op jit(solution)/shard_map/ppermute | solution.py:185
  727.6 23.5 %collective-permute-done.1 = f32[32,32,256]{2,1,0:T(8,128)S(1)} collective-permute-done((f32[32,32,256]{2,1,0:T(8,128)S(1)}, f32[32,32,256]{2,1,0:T(8,128)S(1)}, u32[]{:S(2)}, u32[]{:S(2)}) %collective-permute-start.1) | collective-permute-done | bytes 1048608 | tf_op jit(solution)/shard_map/ppermute | solution.py:185
  751.4 26.1 %collective-permute-done.2 = f32[32,32,256]{2,1,0:T(8,128)S(1)} collective-permute-done((f32[32,32,256]{2,1,0:T(8,128)S(1)}, f32[32,32,256]{2,1,0:T(8,128)S(1)}, u32[]{:S(2)}, u32[]{:S(2)}) %collective-permute-start.2) | collective-permute-done | bytes 1048608 | tf_op jit(solution)/shard_map/ppermute | solution.py:185
  778.2 3.9 collective-permute-start.3
  782.1 2.1 collective-permute-start.4
  784.5 479.5 %collective-permute-done.4 = f32[2,1,4096]{2,1,0:T(1,128)S(1)} collective-permute-done((f32[2,1,4096]{2,1,0:T(1,128)S(1)}, f32[2,1,4096]{2,1,0:T(1,128)S(1)}, u32[]{:S(2)}, u32[]{:S(2)}) %collective-permute-start.4) | collective-permute-done | bytes 32800 | tf_op jit(solution)/shard_map/ppermute | solution.py:22
  1266.8 5.1 collective-permute-start.5
  1273.9 3.9 collective-permute-done.6
  (873 shorter events, 361.9 us)
Async XLA Ops:
  6.5 0.7 copy-start
  6.5 102.5 %copy-start.2 = (s32[32]{0:T(128)S(1)}, s32[32]{0:T(128)}, u32[]{:S(2)}) copy-start(s32[32]{0:T(128)} %param.12) | copy-start | bytes 388
  6.5 102.5 %copy-start.1 = (f32[32]{0:T(128)S(1)}, f32[32]{0:T(128)}, u32[]{:S(2)}) copy-start(f32[32]{0:T(128)} %param.13) | copy-start | bytes 388
  6.5 102.4 %all-gather.4.cloned.1.call-start = ((), (), s32[]{:S(2)}) async-start(), calls=%async_computation | async-start | bytes 8650752 | tf_op jit(solution)/shard_map/all_gather | solution.py:161
  586.7 2.7 collective-permute-start
  589.6 161.5 %collective-permute-start.1 = (f32[32,32,256]{2,1,0:T(8,128)S(1)}, f32[32,32,256]{2,1,0:T(8,128)S(1)}, u32[]{:S(2)}, u32[]{:S(2)}) collective-permute-start(f32[32,32,256]{2,1,0:T(8,128)S(1)} %add.309), channel_id=1, source_target_pairs={{0,64},{32,96},{64,0},{96,32},{128,192},{160,224},{192,128},{224,1... | collective-permute-start | bytes 3145736 | tf_op jit(solution)/shard_map/ppermute | solution.py:185
  751.3 26.2 %collective-permute-start.2 = (f32[32,32,256]{2,1,0:T(8,128)S(1)}, f32[32,32,256]{2,1,0:T(8,128)S(1)}, u32[]{:S(2)}, u32[]{:S(2)}) collective-permute-start(f32[32,32,256]{2,1,0:T(8,128)S(1)} %add.310), channel_id=1, source_target_pairs={{0,128},{32,160},{64,192},{96,224},{128,0},{160,32},{192,64},{224,... | collective-permute-start | bytes 3145736 | tf_op jit(solution)/shard_map/ppermute | solution.py:185
  778.2 6.3 collective-permute-start.3
  782.1 481.8 %collective-permute-start.4 = (f32[2,1,4096]{2,1,0:T(1,128)S(1)}, f32[2,1,4096]{2,1,0:T(1,128)S(1)}, u32[]{:S(2)}, u32[]{:S(2)}) collective-permute-start(f32[2,1,4096]{2,1,0:T(1,128)S(1)} %get-tuple-element.323), channel_id=1, source_target_pairs={{1,0},{2,1},{3,2},{4,3},{5,4},{6,5},{7,6},{8,7},{9,8},{10,9},{11,1... | collective-permute-start | bytes 98312 | tf_op jit(solution)/shard_map/ppermute | solution.py:22
  1266.8 7.1 collective-permute-start.5
  1272.0 5.8 collective-permute-start.6
Sparse Core Ops, SparseCore 0:
  9.9 98.9 all-gather.3
